TPU v7x, 256 devices: a whole 4x4x8 slice. The times are simulated.
256 devices in a mesh: row: 8 (over z), col: 32 (over y, x, core).
Axes of the slice: x: 4, y: 4, z: 8, core: 2. Of those that a mesh axis runs over, the one named last changes fastest.
Arguments:
- tiles: bfloat16 [8, 32, 16, 576, 576], P('row', 'col'), may hold values from -0.0625 to 0.0625
- diag_tiles: bfloat16 [256, 576, 576], P(('row', 'col')), as said below
- probes: float32 [256, 64, 576], P(('row', 'col'))
- rows_list: int32 [8, 32, 16], P('row', 'col'), may hold values from 0 to 31, as said below
- cols_list: int32 [8, 32, 16], P('row', 'col'), may hold values from 0 to 7, as said below
- counts: int32 [8, 32], P('row', 'col'), may hold values from 0 to 16, as said below
Outputs:
- solution: float32 [256, 64, 576], P(('row', 'col'))
- residual: float32 [256, 64, 576], P(('row', 'col'))
Inputs may be any that keep to these rules, and one draw needn't show every extreme that they name: `rows_list`: slots past a device's count hold 0; a held slot lies strictly below the diagonal. `cols_list`: slots past a device's count hold 0. `counts`: the busiest device holds 16 tiles. `diag_tiles`: each diagonal tile is symmetric positive definite: its diagonal entries are at least 4.4 and its off-diagonal part has spectral radius below about 1.
All inputs are finite; a program needn't handle non-finite values.
Results may differ from a plain program's by a relative error of at most 0.039.
Values may be sent and summed in bfloat16 or wider, within the bound.
A program may use at most 128 MiB of HBM per device.

v0:
```python
import jax
import jax.numpy as jnp
from jax import lax
from jax.sharding import PartitionSpec as P

ITERS = 2


def gram_local(left, right):
    return jnp.einsum("tpb,tqb->pq", left, right, precision=lax.Precision.HIGHEST)


def combine(coef, block):
    return jnp.einsum("pq,tpb->tqb", coef, block, precision=lax.Precision.HIGHEST)


def solve_with(matrix, rhs):
    factor = jnp.linalg.cholesky(matrix)
    middle = lax.linalg.triangular_solve(factor, rhs, left_side=True, lower=True, transpose_a=False)
    return lax.linalg.triangular_solve(factor, middle, left_side=True, lower=True, transpose_a=True)


def curvature_sum(direction, image):
    return lax.psum(gram_local(direction, image), ("row", "col"))


def apply_operator(rounded, tiles, diag_tiles, rows_list, cols_list, counts):
    row_probe = lax.all_gather(rounded, "col", axis=0, tiled=True)
    col_probe = lax.all_gather(rounded, "row", axis=0, tiled=True)
    width_p = rounded.shape[1]
    width_b = rounded.shape[2]
    own = lax.dot_general(
        rounded[0], diag_tiles[0], (((1,), (1,)), ((), ())), preferred_element_type=jnp.float32
    )

    def turn(slot, carry):
        acc_row, acc_col = carry
        local = rows_list[0, 0, slot]
        source = cols_list[0, 0, slot]
        block = tiles[0, 0, slot]
        far = col_probe[source]
        near = row_probe[local]
        fwd = lax.dot_general(
            far, block, (((1,), (1,)), ((), ())), preferred_element_type=jnp.float32
        )
        bwd = jnp.dot(near, block, preferred_element_type=jnp.float32)
        return (acc_row.at[local].add(fwd), acc_col.at[source].add(bwd))

    start = (
        jnp.zeros((row_probe.shape[0], width_p, width_b), jnp.float32),
        jnp.zeros((col_probe.shape[0], width_p, width_b), jnp.float32),
    )
    acc_row, acc_col = lax.fori_loop(0, counts[0, 0], turn, start)
    forward = lax.psum_scatter(
        acc_row.astype(jnp.bfloat16), "col", scatter_dimension=0, tiled=True
    ).astype(jnp.float32)
    mirrored = lax.psum_scatter(
        acc_col.astype(jnp.bfloat16), "row", scatter_dimension=0, tiled=True
    ).astype(jnp.float32)
    return forward + mirrored + own[None]


def body(tiles, diag_tiles, probes, rows_list, cols_list, counts):
    solution = jnp.zeros(probes.shape, jnp.float32)
    residual = probes
    direction = probes
    norm_now = lax.psum(gram_local(residual, residual), ("row", "col"))
    for step in range(ITERS):
        image = apply_operator(
            direction.astype(jnp.bfloat16), tiles, diag_tiles, rows_list, cols_list, counts
        )
        final = step + 1 == ITERS
        curv = curvature_sum(direction, image)
        alpha = solve_with(curv, norm_now)
        solution = solution + combine(alpha, direction)
        residual = residual - combine(alpha, image)
        if not final:
            norm_next = lax.psum(gram_local(residual, residual), ("row", "col"))
            beta = solve_with(norm_now, norm_next)
            direction = residual + combine(beta, direction)
            norm_now = norm_next
    return (solution, residual)


def solution(mesh):
    placed = (
        P("row", "col", None, None, None),
        P(("row", "col"), None, None),
        P(("row", "col"), None, None),
        P("row", "col", None),
        P("row", "col", None),
        P("row", "col"),
    )
    return jax.shard_map(
        body,
        mesh=mesh,
        in_specs=placed,
        out_specs=(P(("row", "col"), None, None), P(("row", "col"), None, None)),
        check_vma=False,
    )
```

profile of v0, /device:TPU:1, one launch (start us, length us, event | category | flops | bytes accessed | tf_op | source)
XLA Modules:
  0.0 993.1 jit_solution(8945101122827908853)
XLA Ops:
  9.0 24.3 %all_gather.12 = bf16[8,64,576]{2,1,0:T(8,128)(2,1)S(1)} all-gather(bf16[1,64,576]{2,1,0:T(8,128)(2,1)} %convert_element_type.30), channel_id=1, replica_groups=mesh['row'=8,'col'=32] {'row'}, dimensions={0}, use_global_device_ids=true | all-gather | bytes 663552 | tf_op jit(solution)/shard_map/all_gather | solution.py:29
  33.2 31.7 %all-gather.3.cloned.1.call-done = bf16[32,64,576]{2,1,0:T(8,128)(2,1)} async-done(((bf16[1,64,576]{2,1,0:T(8,128)(2,1)}), bf16[32,64,576]{2,1,0:T(8,128)(2,1)}) %all-gather.3.cloned.1.call-update) | async-done | bytes 2359312 | tf_op jit(solution)/shard_map/all_gather | solution.py:28
  64.9 2.9 broadcast.110.clone
  68.0 22.4 %while.28 = (s32[]{:T(128)}, f32[32,64,576]{2,1,0:T(8,128)}, f32[8,64,576]{2,1,0:T(8,128)S(1)}, s32[]{:T(128)}, s32[1,1,16]{2,1,0:T(1,128)S(1)}, /*index=5*/s32[...) while((s32[]{:T(128)}, f32[32,64,576]{2,1,0:T(8,128)}, ...), condition=%wide.region_3.4_spmd, body=%wide.region_0.3_spmd.sunk | while | flops 85082160 | bytes 2297161 | solution.py:53
  91.4 4.4 convert_element_type.31
  96.3 177.0 %reduce-scatter.7.cloned.1.call-done = bf16[1,64,576]{2,1,0:T(8,128)(2,1)} async-done(((bf16[8,64,576]{2,1,0:T(8,128)(2,1)}), bf16[1,64,576]{2,1,0:T(8,128)(2,1)}) %reduce-scatter.7.cloned.1.call-update) | async-done | bytes 73744 | tf_op jit(solution)/shard_map/reduce_scatter | solution.py:57
  273.2 92.7 %reduce-scatter.5.cloned.1.call-done = bf16[1,64,576]{2,1,0:T(8,128)(2,1)} async-done(((bf16[32,64,576]{2,1,0:T(8,128)(2,1)}), bf16[1,64,576]{2,1,0:T(8,128)(2,1)}) %reduce-scatter.5.cloned.1.call-update) | async-done | bytes 73744 | tf_op jit(solution)/shard_map/reduce_scatter | solution.py:54
  367.5 77.3 %all-reduce = (f32[64,64]{0,1:T(8,128)S(1)}, f32[64,64]{0,1:T(8,128)S(1)}) all-reduce(f32[64,64]{0,1:T(8,128)S(1)} %fusion.49, f32[64,64]{0,1:T(8,128)S(1)} %convolution_bitcast_fusion.10), channel_id=1, replica_groups=mesh['row'=8,'col'=32] {'row','col'}, use_global_device_ids=true, to_apply=%region_9.11 | all-reduce | flops 8192 | bytes 65536 | tf_op jit(solution)/shard_map/psum | solution.py:67
  445.1 5.8 cholesky.70
  452.3 4.9 custom-call.15
  457.1 5.9 cholesky.59
  464.4 4.9 custom-call.13
  470.3 73.9 %psum.30 = f32[64,64]{1,0:T(8,128)S(1)} all-reduce(f32[64,64]{1,0:T(8,128)S(1)} %fusion.45), channel_id=1, replica_groups=mesh['row'=8,'col'=32] {'row','col'}, use_global_device_ids=true, to_apply=%region_10.14 | all-reduce | flops 4096 | bytes 32768 | tf_op jit(solution)/shard_map/psum | solution.py:78
  545.7 20.7 %all_gather.14 = bf16[8,64,576]{2,1,0:T(8,128)(2,1)S(1)} all-gather(bf16[1,64,576]{2,1,0:T(8,128)(2,1)} %get-tuple-element.197), channel_id=1, replica_groups=mesh['row'=8,'col'=32] {'row'}, dimensions={0}, use_global_device_ids=true | all-gather | bytes 663552 | tf_op jit(solution)/shard_map/all_gather | solution.py:29
  566.4 24.9 %all-gather.5.cloned.1.call-done = bf16[32,64,576]{2,1,0:T(8,128)(2,1)} async-done(((bf16[1,64,576]{2,1,0:T(8,128)(2,1)}), bf16[32,64,576]{2,1,0:T(8,128)(2,1)}) %all-gather.5.cloned.1.call-update) | async-done | bytes 2359312 | tf_op jit(solution)/shard_map/all_gather | solution.py:28
  591.3 2.9 broadcast.110
  594.4 22.4 %while.29 = (s32[]{:T(128)}, f32[32,64,576]{2,1,0:T(8,128)}, f32[8,64,576]{2,1,0:T(8,128)S(1)}, s32[]{:T(128)}, s32[1,1,16]{2,1,0:T(1,128)S(1)}, /*index=5*/s32[...) while((s32[]{:T(128)}, f32[32,64,576]{2,1,0:T(8,128)}, ...), condition=%wide.region_14.18_spmd, body=%wide.region_11.17_spmd.sunk | while | flops 85082160 | bytes 2297161 | solution.py:53
  610.7 2.7 fusion.110
  617.8 4.4 convert_element_type.36
  622.6 177.1 %reduce-scatter.11.cloned.1.call-done = bf16[1,64,576]{2,1,0:T(8,128)(2,1)} async-done(((bf16[8,64,576]{2,1,0:T(8,128)(2,1)}), bf16[1,64,576]{2,1,0:T(8,128)(2,1)}) %reduce-scatter.11.cloned.1.call-update) | async-done | bytes 73744 | tf_op jit(solution)/shard_map/reduce_scatter | solution.py:57
  799.7 93.0 %reduce-scatter.9.cloned.1.call-done = bf16[1,64,576]{2,1,0:T(8,128)(2,1)} async-done(((bf16[32,64,576]{2,1,0:T(8,128)(2,1)}), bf16[1,64,576]{2,1,0:T(8,128)(2,1)}) %reduce-scatter.9.cloned.1.call-update) | async-done | bytes 73744 | tf_op jit(solution)/shard_map/reduce_scatter | solution.py:54
  894.3 77.4 %psum.31 = f32[64,64]{0,1:T(8,128)S(1)} all-reduce(f32[64,64]{0,1:T(8,128)S(1)} %fusion.43), channel_id=1, replica_groups=mesh['row'=8,'col'=32] {'row','col'}, use_global_device_ids=true, to_apply=%region_17.21 | all-reduce | flops 4096 | bytes 32768 | tf_op jit(solution)/shard_map/psum | solution.py:24
  971.8 5.8 cholesky.81
  978.9 4.9 custom-call.17
  (83 shorter events, 40.9 us)
Async XLA Ops:
  7.2 358.8 %copy-start = (bf16[1,576,576]{2,1,0:T(8,128)(2,1)S(1)}, bf16[1,576,576]{2,1,0:T(8,128)(2,1)}, u32[]{:S(2)}) copy-start(bf16[1,576,576]{2,1,0:T(8,128)(2,1)} %param.24) | copy-start | bytes 1990660
  7.2 60.8 %copy-start.6 = (s32[3]{0:T(128)S(1)}, s32[3]{0:T(128)}, u32[]{:S(2)}) copy-start(s32[3]{0:T(128)} %constant.124.clone.1) | copy-start | bytes 40
  7.2 60.8 %copy-start.7 = (s32[3]{0:T(128)S(1)}, s32[3]{0:T(128)}, u32[]{:S(2)}) copy-start(s32[3]{0:T(128)} %constant.127.clone.1) | copy-start | bytes 40
  7.2 60.8 %copy-start.4 = (s32[1,1,16]{2,1,0:T(1,128)S(1)}, s32[1,1,16]{2,1,0:T(1,128)}, u32[]{:S(2)}) copy-start(s32[1,1,16]{2,1,0:T(1,128)} %param.26) | copy-start | bytes 196
  7.2 60.8 %copy-start.5 = (s32[1,1,16]{2,1,0:T(1,128)S(1)}, s32[1,1,16]{2,1,0:T(1,128)}, u32[]{:S(2)}) copy-start(s32[1,1,16]{2,1,0:T(1,128)} %param.27) | copy-start | bytes 196
  7.2 57.7 %all-gather.3.cloned.1.call-start = ((), (), s32[]{:S(2)}) async-start(), calls=%async_computation.4 | async-start | bytes 2703360 | tf_op jit(solution)/shard_map/all_gather | solution.py:28
  8.9 264.3 %reduce-scatter.7.cloned.1.call-start = ((), (), s32[]{:S(2)}) async-start(), calls=%async_computation.6 | async-start | bytes 737280 | tf_op jit(solution)/shard_map/reduce_scatter | solution.py:57
  91.4 274.6 %reduce-scatter.5.cloned.1.call-start = ((), (), s32[]{:S(2)}) async-start(), calls=%async_computation.5 | async-start | bytes 2703360 | tf_op jit(solution)/shard_map/reduce_scatter | solution.py:54
  91.4 4.5 copy-start.1
  91.4 274.5 %copy-start.3 = (bf16[1,64,576]{2,1,0:T(8,128)(2,1)S(1)}, bf16[1,64,576]{2,1,0:T(8,128)(2,1)}, u32[]{:S(2)}) copy-start(bf16[1,64,576]{2,1,0:T(8,128)(2,1)} %convert_element_type.30) | copy-start | bytes 221188
  95.9 495.5 %all-gather.5.cloned.1.call-start = ((), (), s32[]{:S(2)}) async-start(), calls=%async_computation.7 | async-start | bytes 2703360 | tf_op jit(solution)/shard_map/all_gather | solution.py:28
  545.6 254.0 %reduce-scatter.11.cloned.1.call-start = ((), (), s32[]{:S(2)}) async-start(), calls=%async_computation.9 | async-start | bytes 737280 | tf_op jit(solution)/shard_map/reduce_scatter | solution.py:57
  617.8 274.9 %reduce-scatter.9.cloned.1.call-start = ((), (), s32[]{:S(2)}) async-start(), calls=%async_computation.8 | async-start | bytes 2703360 | tf_op jit(solution)/shard_map/reduce_scatter | solution.py:54
  617.8 274.9 %copy-start.2 = (bf16[1,64,576]{2,1,0:T(8,128)(2,1)S(1)}, bf16[1,64,576]{2,1,0:T(8,128)(2,1)}, u32[]{:S(2)}) copy-start(bf16[1,64,576]{2,1,0:T(8,128)(2,1)} %get-tuple-element.197) | copy-start | bytes 221188
Sparse Core Ops, SparseCore 0:
  11.2 53.7 all-gather.2
  91.5 181.6 reduce-scatter.6
  277.1 88.7 reduce-scatter.4
  545.8 45.5 all-gather.4
  617.9 181.7 reduce-scatter.10
  803.9 88.7 reduce-scatter.8
where the time goes:
time: 997 us; the launch traced here: 993 us
  waiting for transfers between devices  596 us (60%)
  blocking collectives  274 us (27%)
  other arithmetic  54 us (5%)
  matrix products  27.4 us (3%)
  loops' own time  18.2 us (2%)
  between operations  14.4 us (1%)
    reduce_scatter x2, waiting for transfers between devices, apply_operator(): lax.psum_scatter(acc_col.astype(jnp.bfloat16), 'row', scatter_dimension=0...  354 us
    reduce_scatter x2, waiting for transfers between devices, apply_operator(): lax.psum_scatter(acc_row.astype(jnp.bfloat16), 'col', scatter_dimension=0...  186 us
    psum x1, blocking collectives, curvature_sum(): return lax.psum(gram_local(direction, image), ('row', 'col'))  77.4 us
    psum x1, blocking collectives, body(): norm_now = lax.psum(gram_local(residual, residual), ('row', 'col'))  77.3 us
    psum x1, blocking collectives, body(): norm_next = lax.psum(gram_local(residual, residual), ('row', 'col'))  73.9 us
    all_gather x2, waiting for transfers between devices, apply_operator(): row_probe = lax.all_gather(rounded, 'col', axis=0, tiled=True)  56.6 us
    all_gather x2, blocking collectives, apply_operator(): col_probe = lax.all_gather(rounded, 'row', axis=0, tiled=True)  45 us
  transfers between devices with their start and end apart: 6, of which 6 were waited for; matrix products, arithmetic and copies ran while one was open for 1% of the time, Pallas kernels for 0%

commit v1 on v0

--- a/solution.py
+++ b/solution.py
@@ -75,7 +75,9 @@
         solution = solution + combine(alpha, direction)
         residual = residual - combine(alpha, image)
         if not final:
-            norm_next = lax.psum(gram_local(residual, residual), ("row", "col"))
+            norm_next = jnp.sum(
+                lax.all_gather(gram_local(residual, residual), ("row", "col")), axis=0
+            )
             beta = solve_with(norm_now, norm_next)
             direction = residual + combine(beta, direction)
             norm_now = norm_next

time: 997 us -> 1030 us (1.033)
  waiting for transfers between devices: 596 us -> 702 us
  blocking collectives: 274 us -> 199 us
    all_gather x0 -> x1, waiting for transfers between devices: none -> 103 us  [body(): lax.all_gather(gram_local(residual, residual), ('row', 'col'))]
    psum x1 -> x0, blocking collectives: 73.9 us -> none  [body(): norm_next = lax.psum(gram_local(residual, residual), ('row', 'col'))]
  transfers between devices with their start and end apart: 6 -> 7, of which waited for: 6 -> 7; matrix products, arithmetic and copies ran while one was open for 1% -> 2% of each run, Pallas kernels for 0% -> 0%
where the time goes in v1:
time: 1030 us
  waiting for transfers between devices  702 us (68%)
  blocking collectives  199 us (19%)
  other arithmetic  58 us (6%)
  matrix products  28 us (3%)
  loops' own time  18.2 us (2%)
  between operations  14.4 us (1%)
    reduce_scatter x2, waiting for transfers between devices, apply_operator(): lax.psum_scatter(acc_col.astype(jnp.bfloat16), 'row', scatter_dimension=0...  354 us
    reduce_scatter x2, waiting for transfers between devices, apply_operator(): lax.psum_scatter(acc_row.astype(jnp.bfloat16), 'col', scatter_dimension=0...  186 us
    all_gather x1, waiting for transfers between devices, body(): lax.all_gather(gram_local(residual, residual), ('row', 'col'))  103 us
    psum x1, blocking collectives, curvature_sum(): return lax.psum(gram_local(direction, image), ('row', 'col'))  77.4 us
    psum x1, blocking collectives, body(): norm_now = lax.psum(gram_local(residual, residual), ('row', 'col'))  77.3 us
    all_gather x2, waiting for transfers between devices, apply_operator(): row_probe = lax.all_gather(rounded, 'col', axis=0, tiled=True)  58.2 us
    all_gather x2, blocking collectives, apply_operator(): col_probe = lax.all_gather(rounded, 'row', axis=0, tiled=True)  44.1 us
  transfers between devices with their start and end apart: 7, of which 7 were waited for; matrix products, arithmetic and copies ran while one was open for 2% of the time, Pallas kernels for 0%

profile of v1, /device:TPU:1, one launch (start us, length us, event | category | flops | bytes accessed | tf_op | source)
XLA Modules:
  0.0 1028.3 jit_solution(6147227683289681816)
XLA Ops:
  9.0 24.3 %all_gather.18 = bf16[8,64,576]{2,1,0:T(8,128)(2,1)S(1)} all-gather(bf16[1,64,576]{2,1,0:T(8,128)(2,1)} %convert_element_type.30), channel_id=1, replica_groups=mesh['row'=8,'col'=32] {'row'}, dimensions={0}, use_global_device_ids=true | all-gather | bytes 663552 | tf_op jit(solution)/shard_map/all_gather | solution.py:29
  33.2 31.7 %all-gather.5.cloned.1.call-done = bf16[32,64,576]{2,1,0:T(8,128)(2,1)} async-done(((bf16[1,64,576]{2,1,0:T(8,128)(2,1)}), bf16[32,64,576]{2,1,0:T(8,128)(2,1)}) %all-gather.5.cloned.1.call-update) | async-done | bytes 2359312 | tf_op jit(solution)/shard_map/all_gather | solution.py:28
  64.9 2.9 broadcast.110.clone
  68.0 22.4 %while.28 = (s32[]{:T(128)}, f32[32,64,576]{2,1,0:T(8,128)}, f32[8,64,576]{2,1,0:T(8,128)S(1)}, s32[]{:T(128)}, s32[1,1,16]{2,1,0:T(1,128)S(1)}, /*index=5*/s32[...) while((s32[]{:T(128)}, f32[32,64,576]{2,1,0:T(8,128)}, ...), condition=%wide.region_3.4_spmd, body=%wide.region_0.3_spmd.sunk | while | flops 85082160 | bytes 2297161 | solution.py:53
  91.4 4.4 convert_element_type.31
  96.3 177.0 %reduce-scatter.7.cloned.1.call-done = bf16[1,64,576]{2,1,0:T(8,128)(2,1)} async-done(((bf16[8,64,576]{2,1,0:T(8,128)(2,1)}), bf16[1,64,576]{2,1,0:T(8,128)(2,1)}) %reduce-scatter.7.cloned.1.call-update) | async-done | bytes 73744 | tf_op jit(solution)/shard_map/reduce_scatter | solution.py:57
  273.2 92.7 %reduce-scatter.5.cloned.1.call-done = bf16[1,64,576]{2,1,0:T(8,128)(2,1)} async-done(((bf16[32,64,576]{2,1,0:T(8,128)(2,1)}), bf16[1,64,576]{2,1,0:T(8,128)(2,1)}) %reduce-scatter.5.cloned.1.call-update) | async-done | bytes 73744 | tf_op jit(solution)/shard_map/reduce_scatter | solution.py:54
  367.5 77.3 %all-reduce = (f32[64,64]{0,1:T(8,128)S(1)}, f32[64,64]{0,1:T(8,128)S(1)}) all-reduce(f32[64,64]{0,1:T(8,128)S(1)} %fusion.49, f32[64,64]{0,1:T(8,128)S(1)} %convolution_bitcast_fusion.10), channel_id=1, replica_groups=mesh['row'=8,'col'=32] {'row','col'}, use_global_device_ids=true, to_apply=%region_9.11 | all-reduce | flops 8192 | bytes 65536 | tf_op jit(solution)/shard_map/psum | solution.py:67
  445.1 5.8 cholesky.59
  452.3 4.9 custom-call.13
  458.9 5.8 cholesky.70
  466.1 4.9 custom-call.15
  471.0 103.5 %all-gather.9.cloned.1.call-done = f32[16384,64]{1,0:T(8,128)} async-done(((f32[64,64]{1,0:T(8,128)}), f32[16384,64]{1,0:T(8,128)}) %all-gather.9.cloned.1.call-update) | async-done | bytes 4194320 | tf_op jit(solution)/shard_map/all_gather | solution.py:79
  574.5 4.0 reduce_sum.9
  580.0 19.8 %all_gather.22 = bf16[8,64,576]{2,1,0:T(8,128)(2,1)S(1)} all-gather(bf16[1,64,576]{2,1,0:T(8,128)(2,1)} %get-tuple-element.197), channel_id=1, replica_groups=mesh['row'=8,'col'=32] {'row'}, dimensions={0}, use_global_device_ids=true | all-gather | bytes 663552 | tf_op jit(solution)/shard_map/all_gather | solution.py:29
  599.8 26.5 %all-gather.7.cloned.1.call-done = bf16[32,64,576]{2,1,0:T(8,128)(2,1)} async-done(((bf16[1,64,576]{2,1,0:T(8,128)(2,1)}), bf16[32,64,576]{2,1,0:T(8,128)(2,1)}) %all-gather.7.cloned.1.call-update) | async-done | bytes 2359312 | tf_op jit(solution)/shard_map/all_gather | solution.py:28
  626.3 2.9 broadcast.110
  629.3 22.4 %while.29 = (s32[]{:T(128)}, f32[32,64,576]{2,1,0:T(8,128)}, f32[8,64,576]{2,1,0:T(8,128)S(1)}, s32[]{:T(128)}, s32[1,1,16]{2,1,0:T(1,128)S(1)}, /*index=5*/s32[...) while((s32[]{:T(128)}, f32[32,64,576]{2,1,0:T(8,128)}, ...), condition=%wide.region_14.18_spmd, body=%wide.region_11.17_spmd.sunk | while | flops 85082160 | bytes 2297161 | solution.py:53
  652.8 4.4 convert_element_type.36
  657.5 177.1 %reduce-scatter.11.cloned.1.call-done = bf16[1,64,576]{2,1,0:T(8,128)(2,1)} async-done(((bf16[8,64,576]{2,1,0:T(8,128)(2,1)}), bf16[1,64,576]{2,1,0:T(8,128)(2,1)}) %reduce-scatter.11.cloned.1.call-update) | async-done | bytes 73744 | tf_op jit(solution)/shard_map/reduce_scatter | solution.py:57
  834.6 93.2 %reduce-scatter.9.cloned.1.call-done = bf16[1,64,576]{2,1,0:T(8,128)(2,1)} async-done(((bf16[32,64,576]{2,1,0:T(8,128)(2,1)}), bf16[1,64,576]{2,1,0:T(8,128)(2,1)}) %reduce-scatter.9.cloned.1.call-update) | async-done | bytes 73744 | tf_op jit(solution)/shard_map/reduce_scatter | solution.py:54
  929.4 77.4 %psum.23 = f32[64,64]{0,1:T(8,128)S(1)} all-reduce(f32[64,64]{0,1:T(8,128)S(1)} %fusion.43), channel_id=1, replica_groups=mesh['row'=8,'col'=32] {'row','col'}, use_global_device_ids=true, to_apply=%region_17.21 | all-reduce | flops 4096 | bytes 32768 | tf_op jit(solution)/shard_map/psum | solution.py:24
  1006.9 5.8 cholesky.81
  1014.1 4.9 custom-call.17
  (86 shorter events, 44.3 us)
Async XLA Ops:
  7.2 358.8 %copy-start = (bf16[1,576,576]{2,1,0:T(8,128)(2,1)S(1)}, bf16[1,576,576]{2,1,0:T(8,128)(2,1)}, u32[]{:S(2)}) copy-start(bf16[1,576,576]{2,1,0:T(8,128)(2,1)} %param.24) | copy-start | bytes 1990660
  7.2 60.8 %copy-start.6 = (s32[3]{0:T(128)S(1)}, s32[3]{0:T(128)}, u32[]{:S(2)}) copy-start(s32[3]{0:T(128)} %constant.125.clone.1) | copy-start | bytes 40
  7.2 60.8 %copy-start.7 = (s32[3]{0:T(128)S(1)}, s32[3]{0:T(128)}, u32[]{:S(2)}) copy-start(s32[3]{0:T(128)} %constant.128.clone.1) | copy-start | bytes 40
  7.2 60.8 %copy-start.4 = (s32[1,1,16]{2,1,0:T(1,128)S(1)}, s32[1,1,16]{2,1,0:T(1,128)}, u32[]{:S(2)}) copy-start(s32[1,1,16]{2,1,0:T(1,128)} %param.26) | copy-start | bytes 196
  7.2 60.8 %copy-start.5 = (s32[1,1,16]{2,1,0:T(1,128)S(1)}, s32[1,1,16]{2,1,0:T(1,128)}, u32[]{:S(2)}) copy-start(s32[1,1,16]{2,1,0:T(1,128)} %param.27) | copy-start | bytes 196
  7.2 57.7 %all-gather.5.cloned.1.call-start = ((), (), s32[]{:S(2)}) async-start(), calls=%async_computation.4 | async-start | bytes 2703360 | tf_op jit(solution)/shard_map/all_gather | solution.py:28
  8.9 264.3 %reduce-scatter.7.cloned.1.call-start = ((), (), s32[]{:S(2)}) async-start(), calls=%async_computation.6 | async-start | bytes 737280 | tf_op jit(solution)/shard_map/reduce_scatter | solution.py:57
  91.4 274.6 %reduce-scatter.5.cloned.1.call-start = ((), (), s32[]{:S(2)}) async-start(), calls=%async_computation.5 | async-start | bytes 2703360 | tf_op jit(solution)/shard_map/reduce_scatter | solution.py:54
  91.4 4.5 copy-start.1
  91.4 274.5 %copy-start.3 = (bf16[1,64,576]{2,1,0:T(8,128)(2,1)S(1)}, bf16[1,64,576]{2,1,0:T(8,128)(2,1)}, u32[]{:S(2)}) copy-start(bf16[1,64,576]{2,1,0:T(8,128)(2,1)} %convert_element_type.30) | copy-start | bytes 221188
  95.9 478.6 %all-gather.9.cloned.1.call-start = ((), (), s32[]{:S(2)}) async-start(), calls=%async_computation.10 | async-start | bytes 8421376 | tf_op jit(solution)/shard_map/all_gather | solution.py:79
  458.9 167.4 %all-gather.7.cloned.1.call-start = ((), (), s32[]{:S(2)}) async-start(), calls=%async_computation.7 | async-start | bytes 2703360 | tf_op jit(solution)/shard_map/all_gather | solution.py:28
  579.9 254.7 %reduce-scatter.11.cloned.1.call-start = ((), (), s32[]{:S(2)}) async-start(), calls=%async_computation.9 | async-start | bytes 737280 | tf_op jit(solution)/shard_map/reduce_scatter | solution.py:57
  652.7 275.1 %reduce-scatter.9.cloned.1.call-start = ((), (), s32[]{:S(2)}) async-start(), calls=%async_computation.8 | async-start | bytes 2703360 | tf_op jit(solution)/shard_map/reduce_scatter | solution.py:54
  652.8 275.0 %copy-start.2 = (bf16[1,64,576]{2,1,0:T(8,128)(2,1)S(1)}, bf16[1,64,576]{2,1,0:T(8,128)(2,1)}, u32[]{:S(2)}) copy-start(bf16[1,64,576]{2,1,0:T(8,128)(2,1)} %get-tuple-element.197) | copy-start | bytes 221188
Sparse Core Ops, SparseCore 0:
  11.2 53.7 all-gather.4
  91.5 181.6 reduce-scatter.6
  277.1 88.7 reduce-scatter.4
  459.0 115.4 all-gather.8
  580.1 46.2 all-gather.6
  652.8 181.7 reduce-scatter.10
  839.0 88.7 reduce-scatter.8
